TPU v7x, 128 devices: a whole 4x4x4 slice. The times are simulated.
128 devices in a mesh: row: 8 (over x_lo, z), col: 16 (over y, x_hi, core).
Axes of the slice: x: 4 (x_hi: 2, x_lo: 2; x = x_hi * 2 + x_lo), y: 4, z: 4, core: 2. Of those that a mesh axis runs over, the one named last changes fastest.
Arguments:
- tokens: bfloat16 [1024, 12288], P('col', 'row'), may hold values from -6 to 6
- up_weight: bfloat16 [12288, 24576], P('row', 'col'), may hold values from -0.109375 to 0.109375
- up_mask: int32 [192, 384], P('row', 'col'), may hold values 0 or 1
- down_weight: bfloat16 [24576, 12288], P('col', 'row'), may hold values from -0.078125 to 0.078125
- down_mask: int32 [384, 192], P('col', 'row'), may hold values 0 or 1
- grad_out: bfloat16 [1024, 12288], P('col', 'row'), may hold values from -6 to 6
Outputs:
- out_heads: bfloat16 [96, 1024, 128], P('row', 'col')
- grad_tokens: bfloat16 [1024, 12288], P('col', 'row')
- grad_up: bfloat16 [12288, 24576], P('row', 'col')
- grad_down: bfloat16 [24576, 12288], P('col', 'row')
All inputs are finite; a program needn't handle non-finite values. No bound on the sum of `up_mask` or of `down_mask` on one device may be relied on, other than what follows from the above.
Results may differ from a plain program's by a relative error of at most 0.022.
Values may be sent and summed in bfloat16 or wider, within the bound.
A program may use at most 192 MiB of HBM per device.

v0:
```python
import math
import jax
import jax.numpy as jnp
from jax import lax
from jax.sharding import PartitionSpec as P

BLOCK = 64
HEAD_DIM = 128


def expand(weight, mask):
    rows_in, cols_in = weight.shape
    tiles = weight.reshape(rows_in // BLOCK, BLOCK, cols_in // BLOCK, BLOCK)
    tiles = tiles * mask.astype(weight.dtype)[:, None, :, None]
    return tiles.reshape(rows_in, cols_in)


def activate(value):
    return jax.nn.gelu(value, approximate=True)


def times_transposed(left, right):
    return lax.dot_general(
        left, right, (((1,), (1,)), ((), ())), preferred_element_type=jnp.float32
    )


def over_tokens(left, right):
    return lax.dot_general(
        left, right, (((0,), (0,)), ((), ())), preferred_element_type=jnp.float32
    )


def body(tokens, up_weight, up_mask, down_weight, down_mask, grad_out):
    w_up = expand(up_weight, up_mask)
    w_down = expand(down_weight, down_mask)
    tok_all = lax.all_gather(tokens, "col", axis=0, tiled=True)
    token_count = tok_all.shape[0]
    col_share = token_count // lax.axis_size("col")
    piece = tok_all
    pre_act = lax.psum_scatter(
        jnp.dot(piece, w_up, preferred_element_type=jnp.float32).astype(jnp.bfloat16),
        "row",
        scatter_dimension=0,
        tiled=True,
    ).astype(jnp.float32)
    hidden = activate(pre_act).astype(jnp.bfloat16)
    hidden_all = lax.all_gather(hidden, "row", axis=0, tiled=True)
    piece = hidden_all
    output_rows = lax.psum_scatter(
        jnp.dot(piece, w_down, preferred_element_type=jnp.float32).astype(jnp.bfloat16),
        "col",
        scatter_dimension=0,
        tiled=True,
    )
    out_heads = output_rows.reshape(
        col_share, output_rows.shape[1] // HEAD_DIM, HEAD_DIM
    ).transpose(1, 0, 2)
    cot_all = lax.all_gather(grad_out, "col", axis=0, tiled=True)
    piece = cot_all
    grad_hidden = lax.psum_scatter(
        times_transposed(piece, w_down).astype(jnp.bfloat16), "row", scatter_dimension=0, tiled=True
    ).astype(jnp.float32)
    unused, pull = jax.vjp(activate, pre_act)
    grad_pre = pull(grad_hidden)[0].astype(jnp.bfloat16)
    grad_pre_all = lax.all_gather(grad_pre, "row", axis=0, tiled=True)
    grad_scale = 1.0 / math.sqrt(token_count)
    grad_up = expand(over_tokens(tok_all, grad_pre_all) * grad_scale, up_mask).astype(jnp.bfloat16)
    grad_down = expand(over_tokens(hidden_all, cot_all) * grad_scale, down_mask).astype(
        jnp.bfloat16
    )
    piece = grad_pre_all
    grad_tokens = lax.psum_scatter(
        times_transposed(piece, w_up).astype(jnp.bfloat16), "col", scatter_dimension=0, tiled=True
    )
    return (out_heads, grad_tokens, grad_up, grad_down)


def solution(mesh):
    return jax.shard_map(
        body,
        mesh=mesh,
        in_specs=(
            P("col", "row"),
            P("row", "col"),
            P("row", "col"),
            P("col", "row"),
            P("col", "row"),
            P("col", "row"),
        ),
        out_specs=(P("row", "col", None), P("col", "row"), P("row", "col"), P("col", "row")),
        check_vma=False,
    )
```

profile of v0, /device:TPU:0, one launch (start us, length us, event | category | flops | bytes accessed | tf_op | source)
XLA Modules:
  0.0 489.4 jit_solution(12928435325429374456)
XLA Ops:
  7.2 0.0 all-gather.9.cloned.1.call-start
  7.2 0.7 all-gather.9.cloned.1.call-update
  7.9 0.0 all-gather.5.cloned.1.call-start
  7.9 0.7 all-gather.5.cloned.1.call-update
  8.6 0.0 reduce-scatter.15.cloned.1.call-start
  8.7 0.8 fusion.18
  9.5 4.9 %mul.107 = bf16[24,64,24,64]{3,2,1,0:T(8,128)(2,1)} broadcast(bf16[24,24]{1,0:T(8,128)(2,1)S(1)} %get-tuple-element.19), dimensions={0,2} | broadcast | bytes 4719744 | tf_op jit(solution)/shard_map/mul | solution.py:14
  14.4 13.1 %mul.108 = bf16[1536,1536]{1,0:T(8,128)(2,1)} reshape(bf16[24,64,24,64]{3,2,1,0:T(8,128)(2,1)} %mul.107) | data formatting | bytes 9437184 | tf_op jit(solution)/shard_map/mul | solution.py:14
  27.5 35.9 %all-gather.9.cloned.1.call-done = bf16[1024,1536]{1,0:T(8,128)(2,1)} async-done(((bf16[64,1536]{1,0:T(8,128)(2,1)}), bf16[1024,1536]{1,0:T(8,128)(2,1)}) %all-gather.9.cloned.1.call-update) | async-done | bytes 3145744 | tf_op jit(solution)/shard_map/all_gather | solution.py:59
  63.4 9.5 %fusion.4 = bf16[1024,1536]{0,1:T(8,128)(2,1)S(1)} fusion(bf16[1024,1536]{1,0:T(8,128)(2,1)} %all-gather.9.cloned.1.call-done, bf16[1536,1536]{1,0:T(8,128)(2,1)} %param.9, bf16[1536,1536]{1,0:T(8,128)(2,1)} %mul.108), kind=kOutput, calls=%fused_computation.11 | convolution fusion | flops 4835770368 | bytes 15728640 | tf_op jit(solution)/shard_map/dot_general | solution.py:23
  72.9 0.0 copy-start
  73.0 2.9 copy.21
  75.9 0.0 reduce-scatter.15.cloned.1.call-update
  75.9 0.2 reduce-scatter.13.cloned.1.call-start
  76.1 0.0 copy-done
  76.2 4.9 %mul.100 = bf16[24,64,24,64]{3,2,1,0:T(8,128)(2,1)} broadcast(bf16[24,24]{1,0:T(8,128)(2,1)S(1)} %get-tuple-element.21), dimensions={0,2} | broadcast | bytes 4719744 | tf_op jit(solution)/shard_map/mul | solution.py:14
  81.1 13.0 %mul.101 = bf16[1536,1536]{1,0:T(8,128)(2,1)} reshape(bf16[24,64,24,64]{3,2,1,0:T(8,128)(2,1)} %mul.100) | data formatting | bytes 9437184 | tf_op jit(solution)/shard_map/mul | solution.py:14
  94.2 7.6 %mul.102 = bf16[1536,1536]{1,0:T(8,128)(2,1)} multiply(bf16[1536,1536]{1,0:T(8,128)(2,1)} %param.7, bf16[1536,1536]{1,0:T(8,128)(2,1)} %mul.101) | non-fusion elementwise | flops 2359296 | bytes 14155776 | tf_op jit(solution)/shard_map/mul | solution.py:14
  101.8 13.4 %all-gather.5.cloned.1.call-done = bf16[1024,1536]{1,0:T(8,128)(2,1)} async-done(((bf16[64,1536]{1,0:T(8,128)(2,1)}), bf16[1024,1536]{1,0:T(8,128)(2,1)}) %all-gather.5.cloned.1.call-update) | async-done | bytes 3145744 | tf_op jit(solution)/shard_map/all_gather | solution.py:37
  115.2 8.2 %fusion.3 = bf16[1024,1536]{0,1:T(8,128)(2,1)S(1)} fusion(bf16[1536,1536]{1,0:T(8,128)(2,1)} %mul.102, bf16[1024,1536]{1,0:T(8,128)(2,1)} %all-gather.5.cloned.1.call-done), kind=kOutput, calls=%fused_computation.10 | convolution fusion | flops 4833411072 | bytes 11010048 | tf_op jit(solution)/shard_map/dot_general | solution.py:42
  123.4 3.0 copy.19
  126.3 0.0 reduce-scatter.13.cloned.1.call-update
  126.3 0.0 all-gather.7.cloned.1.call-start
  126.4 36.6 %reduce-scatter.15.cloned.1.call-done = bf16[128,1536]{1,0:T(8,128)(2,1)} async-done(((bf16[1024,1536]{1,0:T(8,128)(2,1)}), bf16[128,1536]{1,0:T(8,128)(2,1)}) %reduce-scatter.15.cloned.1.call-update) | async-done | bytes 393232
  163.0 1.2 copy.22
  164.3 47.4 %reduce-scatter.13.cloned.1.call-done = bf16[128,1536]{1,0:T(8,128)(2,1)} async-done(((bf16[1024,1536]{1,0:T(8,128)(2,1)}), bf16[128,1536]{1,0:T(8,128)(2,1)}) %reduce-scatter.13.cloned.1.call-update) | async-done | bytes 393232
  211.7 1.2 copy.20
  212.9 1.5 fusion.10
  214.4 0.0 all-gather.7.cloned.1.call-update
  214.5 0.0 all-gather.11.cloned.1.call-start
  214.5 0.5 all-gather.11.cloned.1.call-update
  215.0 0.0 reduce-scatter.9.cloned.1.call-start
  215.1 51.8 %all-gather.7.cloned.1.call-done = bf16[1024,1536]{0,1:T(8,128)(2,1)} async-done(((bf16[128,1536]{0,1:T(8,128)(2,1)}), bf16[1024,1536]{0,1:T(8,128)(2,1)}) %all-gather.7.cloned.1.call-update) | async-done | bytes 3145744 | tf_op jit(solution)/shard_map/all_gather | solution.py:48
  266.9 10.7 %convolution_convert_fusion.2 = bf16[1024,1536]{1,0:T(8,128)(2,1)} fusion(bf16[1024,1536]{0,1:T(8,128)(2,1)} %all-gather.7.cloned.1.call-done, bf16[1536,1536]{1,0:T(8,128)(2,1)} %param.9, bf16[1536,1536]{1,0:T(8,128)(2,1)} %mul.108), kind=kOutput, calls=%fused_computation.8 | convolution fusion | flops 4835770368 | bytes 15728640 | tf_op jit(solution)/shard_map/dot_general | solution.py:51
  277.6 0.0 reduce-scatter.9.cloned.1.call-update
  277.6 0.3 reduce-scatter.11.cloned.1.call-start
  277.9 45.0 %all-gather.11.cloned.1.call-done = bf16[1024,1536]{0,1:T(8,128)(2,1)} async-done(((bf16[128,1536]{0,1:T(8,128)(2,1)}), bf16[1024,1536]{0,1:T(8,128)(2,1)}) %all-gather.11.cloned.1.call-update) | async-done | bytes 3145744 | tf_op jit(solution)/shard_map/all_gather | solution.py:66
  322.8 9.3 %convolution_convert_fusion = bf16[1024,1536]{1,0:T(8,128)(2,1)} fusion(bf16[1024,1536]{0,1:T(8,128)(2,1)} %all-gather.11.cloned.1.call-done, bf16[1536,1536]{1,0:T(8,128)(2,1)} %mul.102), kind=kOutput, calls=%fused_computation.6 | convolution fusion | flops 4833411072 | bytes 11010048 | tf_op jit(solution)/shard_map/dot_general | solution.py:23
  332.1 0.0 reduce-scatter.11.cloned.1.call-update
  332.1 0.1 copy.16
  332.2 8.1 %mul.127 = f32[24,64,24,64]{3,2,1,0:T(8,128)} broadcast(f32[24,24]{1,0:T(8,128)S(1)} %get-tuple-element.18), dimensions={0,2} | broadcast | bytes 9439488 | tf_op jit(solution)/shard_map/mul | solution.py:14
  340.3 16.6 %mul.128 = f32[1536,1536]{1,0:T(8,128)} reshape(f32[24,64,24,64]{3,2,1,0:T(8,128)} %mul.127) | data formatting | bytes 18874368 | tf_op jit(solution)/shard_map/mul | solution.py:14
  356.9 7.9 %mul.123 = f32[24,64,24,64]{1,0,3,2:T(8,128)} broadcast(f32[24,24]{0,1:T(8,128)S(1)} %copy.16), dimensions={0,2} | broadcast | bytes 9439488 | tf_op jit(solution)/shard_map/mul | solution.py:14
  364.8 0.0 copy-start.2
  364.8 16.5 %mul.124 = f32[1536,1536]{0,1:T(8,128)} reshape(f32[24,64,24,64]{1,0,3,2:T(8,128)} %mul.123) | data formatting | bytes 18874368 | tf_op jit(solution)/shard_map/mul | solution.py:14
  381.4 0.0 copy-done.2
  381.4 10.0 %fusion.1 = bf16[1536,1536]{0,1:T(8,128)(2,1)} fusion(f32[1536,1536]{0,1:T(8,128)} %mul.124, bf16[1024,1536]{0,1:T(8,128)(2,1)} %all-gather.11.cloned.1.call-done, bf16[1024,1536]{1,0:T(8,128)(2,1)S(1)} %copy-done.2), kind=kOutput, calls=%fused_computation.4 | convolution fusion | flops 4838916096 | bytes 20447232 | tf_op jit(solution)/shard_map/dot_general | solution.py:29
  391.4 0.0 copy-start.1
  391.4 6.8 %copy.18 = bf16[1536,1536]{1,0:T(8,128)(2,1)} copy(bf16[1536,1536]{0,1:T(8,128)(2,1)} %fusion.1) | data formatting | bytes 9437184
  398.2 0.0 copy-done.1
  398.2 10.1 %fusion.2 = bf16[1536,1536]{1,0:T(8,128)(2,1)} fusion(f32[1536,1536]{1,0:T(8,128)} %mul.128, bf16[1024,1536]{0,1:T(8,128)(2,1)} %all-gather.7.cloned.1.call-done, bf16[1024,1536]{1,0:T(8,128)(2,1)S(1)} %copy-done.1), kind=kOutput, calls=%fused_computation.5 | convolution fusion | flops 4838916096 | bytes 20447232 | tf_op jit(solution)/shard_map/dot_general | solution.py:29
  408.3 0.0 reduce-scatter.9.cloned.1.call-done
  408.3 1.1 reshape.27
  409.4 0.7 copy.17
  410.1 72.4 %reduce-scatter.11.cloned.1.call-done = bf16[64,1536]{1,0:T(8,128)(2,1)} async-done(((bf16[1024,1536]{1,0:T(8,128)(2,1)}), bf16[64,1536]{1,0:T(8,128)(2,1)}) %reduce-scatter.11.cloned.1.call-update) | async-done | bytes 196624 | tf_op jit(solution)/shard_map/reduce_scatter | solution.py:73
  (1 shorter events, 0.0 us)
Async XLA Ops:
  7.2 56.2 %all-gather.9.cloned.1.call-start = ((), (), s32[]{:S(2)}) async-start(), calls=%async_computation.7 | async-start | bytes 3342336 | tf_op jit(solution)/shard_map/all_gather | solution.py:59
  7.9 107.3 %all-gather.5.cloned.1.call-start = ((), (), s32[]{:S(2)}) async-start(), calls=%async_computation.4 | async-start | bytes 3342336 | tf_op jit(solution)/shard_map/all_gather | solution.py:37
  8.6 154.4 %reduce-scatter.15.cloned.1.call-start = ((), (), s32[]{:S(2)}) async-start(), calls=%async_computation.11 | async-start | bytes 3538944
  72.9 3.2 copy-start
  75.9 135.8 %reduce-scatter.13.cloned.1.call-start = ((), (), s32[]{:S(2)}) async-start(), calls=%async_computation.10 | async-start | bytes 3538944
  126.3 140.5 %all-gather.7.cloned.1.call-start = ((), (), s32[]{:S(2)}) async-start(), calls=%async_computation.5 | async-start | bytes 3538944 | tf_op jit(solution)/shard_map/all_gather | solution.py:48
  214.5 108.4 %all-gather.11.cloned.1.call-start = ((), (), s32[]{:S(2)}) async-start(), calls=%async_computation.8 | async-start | bytes 3538944 | tf_op jit(solution)/shard_map/all_gather | solution.py:66
  215.0 193.3 %reduce-scatter.9.cloned.1.call-start = ((), (), s32[]{:S(2)}) async-start(), calls=%async_computation.6 | async-start | bytes 3342336 | tf_op jit(solution)/shard_map/reduce_scatter | solution.py:50
  277.6 205.0 %reduce-scatter.11.cloned.1.call-start = ((), (), s32[]{:S(2)}) async-start(), calls=%async_computation.9 | async-start | bytes 3342336 | tf_op jit(solution)/shard_map/reduce_scatter | solution.py:73
  364.8 16.6 %copy-start.2 = (bf16[1024,1536]{1,0:T(8,128)(2,1)S(1)}, bf16[1024,1536]{1,0:T(8,128)(2,1)}, u32[]{:S(2)}) copy-start(bf16[1024,1536]{1,0:T(8,128)(2,1)} %all-gather.5.cloned.1.call-done) | copy-start | bytes 9437188
  391.4 6.8 %copy-start.1 = (bf16[1024,1536]{1,0:T(8,128)(2,1)S(1)}, bf16[1024,1536]{1,0:T(8,128)(2,1)}, u32[]{:S(2)}) copy-start(bf16[1024,1536]{1,0:T(8,128)(2,1)} %all-gather.9.cloned.1.call-done) | copy-start | bytes 9437188
Sparse Core Ops, SparseCore 0:
  10.4 52.9 all-gather.8
  65.9 49.2 all-gather.4
  117.6 45.3 reduce-scatter.14
  165.3 46.3 reduce-scatter.12
  214.6 52.2 all-gather.6
  268.3 54.4 all-gather.10
  326.9 76.7 reduce-scatter.8
  408.3 74.1 reduce-scatter.10
where the time goes:
time: 491 us; the launch traced here: 489 us
  waiting for transfers between devices  305 us (62%)
  local copies, waits for them, and re-layouts  102 us (21%)
  matrix products  57.8 us (12%)
  between operations  14.2 us (3%)
  other arithmetic  9.97 us (2%)
    unnamed x10, waiting for transfers between devices  86 us
    mul x8, local copies, waits for them, and re-layouts, expand(): tiles = tiles * mask.astype(weight.dtype)[:, None, :, None]  85.2 us
    reduce_scatter x1, waiting for transfers between devices, body(): lax.psum_scatter(times_transposed(piece, w_up).astype(jnp.bfloat16), 'col...  72.4 us
    all_gather x1, waiting for transfers between devices, body(): hidden_all = lax.all_gather(hidden, 'row', axis=0, tiled=True)  51.8 us
    all_gather x1, waiting for transfers between devices, body(): grad_pre_all = lax.all_gather(grad_pre, 'row', axis=0, tiled=True)  45 us
    all_gather x1, waiting for transfers between devices, body(): cot_all = lax.all_gather(grad_out, 'col', axis=0, tiled=True)  35.9 us
    dot_general x2, matrix products, over_tokens(): lax.dot_general(left, right, (((0,), (0,)), ((), ())), preferred_element_...  20.1 us
    dot_general x2, matrix products, times_transposed(): lax.dot_general(left, right, (((1,), (1,)), ((), ())), preferred_element_...  18.8 us
  transfers between devices with their start and end apart: 8, of which 7 were waited for; matrix products, arithmetic and copies ran while one was open for 34% of the time, Pallas kernels for 0%

commit v1 on v0

--- a/solution.py
+++ b/solution.py
@@ -56,7 +56,9 @@
     out_heads = output_rows.reshape(
         col_share, output_rows.shape[1] // HEAD_DIM, HEAD_DIM
     ).transpose(1, 0, 2)
-    cot_all = lax.all_gather(grad_out, "col", axis=0, tiled=True)
+    cot_all = jnp.concatenate(
+        lax.all_to_all(jnp.stack([grad_out] * lax.axis_size("col")), "col", 0, 0), axis=0
+    )
     piece = cot_all
     grad_hidden = lax.psum_scatter(
         times_transposed(piece, w_down).astype(jnp.bfloat16), "row", scatter_dimension=0, tiled=True

time: 491 us -> 404 us (0.82)
  waiting for transfers between devices: 305 us -> 199 us
  starting transfers between devices: 0.72 us -> 7.84 us
  local copies, waits for them, and re-layouts: 102 us -> 109 us
    reduce_scatter x1, waiting for transfers between devices: 72.4 us -> 19.2 us  [body(): lax.psum_scatter(times_transposed(piece, w_up).astype(jnp.bfloat16), 'col...]
    all_gather x1 -> x0, waiting for transfers between devices: 35.9 us -> none  [body(): cot_all = lax.all_gather(grad_out, 'col', axis=0, tiled=True)]
    unnamed x10 -> x9, waiting for transfers between devices: 86 us -> 53 us
    all_to_all x0 -> x1, waiting for transfers between devices: none -> 24.5 us  [body(): lax.all_to_all(jnp.stack([grad_out] * lax.axis_size('col')), 'col', 0, 0)]
    all_gather x1, waiting for transfers between devices: 13.4 us -> 0.01 us  [body(): tok_all = lax.all_gather(tokens, 'col', axis=0, tiled=True)]
    all_to_all x0 -> x1, starting transfers between devices: none -> 7.15 us  [body(): lax.all_to_all(jnp.stack([grad_out] * lax.axis_size('col')), 'col', 0, 0)]
    all_gather x1, waiting for transfers between devices: 45 us -> 50.7 us  [body(): grad_pre_all = lax.all_gather(grad_pre, 'row', axis=0, tiled=True)]
  transfers between devices with their start and end apart: 8 -> 8, of which waited for: 7 -> 6; matrix products, arithmetic and copies ran while one was open for 34% -> 44% of each run, Pallas kernels for 0% -> 0%
where the time goes in v1:
time: 404 us; the launch traced here: 402 us
  waiting for transfers between devices  199 us (49%)
  local copies, waits for them, and re-layouts  109 us (27%)
  matrix products  60.8 us (15%)
  between operations  15.5 us (4%)
  other arithmetic  10.5 us (3%)
  starting transfers between devices  7.84 us (2%)
    mul x8, local copies, waits for them, and re-layouts, expand(): tiles = tiles * mask.astype(weight.dtype)[:, None, :, None]  84.6 us
    unnamed x9, waiting for transfers between devices  53 us
    all_gather x1, waiting for transfers between devices, body(): hidden_all = lax.all_gather(hidden, 'row', axis=0, tiled=True)  51.8 us
    all_gather x1, waiting for transfers between devices, body(): grad_pre_all = lax.all_gather(grad_pre, 'row', axis=0, tiled=True)  50.7 us
    all_to_all x1, waiting for transfers between devices, body(): lax.all_to_all(jnp.stack([grad_out] * lax.axis_size('col')), 'col', 0, 0)  24.5 us
    dot_general x2, matrix products, over_tokens(): lax.dot_general(left, right, (((0,), (0,)), ((), ())), preferred_element_...  20.5 us
    dot_general x2, matrix products, times_transposed(): lax.dot_general(left, right, (((1,), (1,)), ((), ())), preferred_element_...  20.1 us
    unnamed x12, local copies, waits for them, and re-layouts  19.8 us
  transfers between devices with their start and end apart: 8, of which 6 were waited for; matrix products, arithmetic and copies ran while one was open for 44% of the time, Pallas kernels for 0%

profile of v1, /device:TPU:0, one launch (start us, length us, event | category | flops | bytes accessed | tf_op | source)
XLA Modules:
  0.0 402.4 jit_solution(2354749235322496909)
XLA Ops:
  8.0 0.0 all-gather.4.cloned.1.call-start
  8.0 0.7 all-gather.4.cloned.1.call-update
  8.7 0.0 copy-start.1
  8.7 2.9 stack.2
  11.6 7.1 %all-to-all-start = ((bf16[16,64,1536]{2,1,0:T(8,128)(2,1)}), bf16[16,64,1536]{2,1,0:T(8,128)(2,1)S(1)}, u32[]{:S(2)}, u32[]{:S(2)}) async-start(bf16[16,64,1536]{2,1,0:T(8,128)(2,1)} %stack.2), calls=%async_computation.1 | async-start | bytes 6291456 | tf_op jit(solution)/shard_map/all_to_all | solution.py:60
  18.8 0.0 reduce-scatter.15.cloned.1.call-start
  18.8 0.0 copy-done.1
  18.9 4.9 %mul.107 = bf16[24,64,24,64]{3,2,1,0:T(8,128)(2,1)} broadcast(bf16[24,24]{1,0:T(8,128)(2,1)S(1)} %get-tuple-element.19), dimensions={0,2} | broadcast | bytes 4719744 | tf_op jit(solution)/shard_map/mul | solution.py:14
  23.8 13.1 %mul.108 = bf16[1536,1536]{1,0:T(8,128)(2,1)} reshape(bf16[24,64,24,64]{3,2,1,0:T(8,128)(2,1)} %mul.107) | data formatting | bytes 9437184 | tf_op jit(solution)/shard_map/mul | solution.py:14
  36.9 24.5 %all-to-all-done = bf16[16,64,1536]{2,1,0:T(8,128)(2,1)S(1)} async-done(((bf16[16,64,1536]{2,1,0:T(8,128)(2,1)}), bf16[16,64,1536]{2,1,0:T(8,128)(2,1)S(1)}, u32[]{:S(2)}, u32[]{:S(2)}) %all-to-all-start) | async-done | bytes 3145760 | tf_op jit(solution)/shard_map/all_to_all | solution.py:60
  61.4 10.6 %fusion.4 = bf16[1024,1536]{0,1:T(8,128)(2,1)} fusion(bf16[1024,1536]{1,0:T(8,128)(2,1)S(1)} %bitcast.32, bf16[1536,1536]{1,0:T(8,128)(2,1)} %param.9, bf16[1536,1536]{1,0:T(8,128)(2,1)} %mul.108), kind=kOutput, calls=%fused_computation.11 | convolution fusion | flops 4835770368 | bytes 15728640 | tf_op jit(solution)/shard_map/dot_general | solution.py:23
  72.0 0.0 copy-start.2
  72.0 4.7 %copy.21 = bf16[1024,1536]{1,0:T(8,128)(2,1)} copy(bf16[1024,1536]{0,1:T(8,128)(2,1)} %fusion.4) | data formatting | bytes 6291456
  76.7 0.0 reduce-scatter.15.cloned.1.call-update
  76.7 0.2 reduce-scatter.13.cloned.1.call-start
  76.9 0.0 copy-done.2
  76.9 0.6 fusion.19
  77.5 4.9 %mul.100 = bf16[24,64,24,64]{3,2,1,0:T(8,128)(2,1)} broadcast(bf16[24,24]{1,0:T(8,128)(2,1)S(1)} %get-tuple-element.21), dimensions={0,2} | broadcast | bytes 4719744 | tf_op jit(solution)/shard_map/mul | solution.py:14
  82.5 13.1 %mul.101 = bf16[1536,1536]{1,0:T(8,128)(2,1)} reshape(bf16[24,64,24,64]{3,2,1,0:T(8,128)(2,1)} %mul.100) | data formatting | bytes 9437184 | tf_op jit(solution)/shard_map/mul | solution.py:14
  95.5 7.3 %mul.102 = bf16[1536,1536]{1,0:T(8,128)(2,1)} multiply(bf16[1536,1536]{1,0:T(8,128)(2,1)} %param.7, bf16[1536,1536]{1,0:T(8,128)(2,1)} %mul.101) | non-fusion elementwise | flops 2359296 | bytes 14155776 | tf_op jit(solution)/shard_map/mul | solution.py:14
  102.9 0.0 all-gather.4.cloned.1.call-done
  102.9 9.5 %fusion.3 = bf16[1024,1536]{0,1:T(8,128)(2,1)} fusion(bf16[1536,1536]{1,0:T(8,128)(2,1)} %mul.102, bf16[1024,1536]{1,0:T(8,128)(2,1)} %all-gather.4.cloned.1.call-done), kind=kOutput, calls=%fused_computation.10 | convolution fusion | flops 4833411072 | bytes 11010048 | tf_op jit(solution)/shard_map/dot_general | solution.py:42
  112.4 4.7 %copy.19 = bf16[1024,1536]{1,0:T(8,128)(2,1)} copy(bf16[1024,1536]{0,1:T(8,128)(2,1)} %fusion.3) | data formatting | bytes 6291456
  117.1 0.0 reduce-scatter.13.cloned.1.call-update
  117.1 0.0 all-gather.6.cloned.1.call-start
  117.2 4.5 %reduce-scatter.15.cloned.1.call-done = bf16[128,1536]{1,0:T(8,128)(2,1)} async-done(((bf16[1024,1536]{1,0:T(8,128)(2,1)}), bf16[128,1536]{1,0:T(8,128)(2,1)}) %reduce-scatter.15.cloned.1.call-update) | async-done | bytes 393232
  121.6 1.2 copy.22
  122.9 47.0 %reduce-scatter.13.cloned.1.call-done = bf16[128,1536]{1,0:T(8,128)(2,1)} async-done(((bf16[1024,1536]{1,0:T(8,128)(2,1)}), bf16[128,1536]{1,0:T(8,128)(2,1)}) %reduce-scatter.13.cloned.1.call-update) | async-done | bytes 393232
  169.9 1.9 copy.20
  171.8 2.6 fusion.10
  174.4 0.0 all-gather.6.cloned.1.call-update
  174.4 0.0 all-gather.8.cloned.1.call-start
  174.5 0.7 all-gather.8.cloned.1.call-update
  175.2 0.0 reduce-scatter.9.cloned.1.call-start
  175.2 51.8 %all-gather.6.cloned.1.call-done = bf16[1024,1536]{0,1:T(8,128)(2,1)} async-done(((bf16[128,1536]{0,1:T(8,128)(2,1)}), bf16[1024,1536]{0,1:T(8,128)(2,1)}) %all-gather.6.cloned.1.call-update) | async-done | bytes 3145744 | tf_op jit(solution)/shard_map/all_gather | solution.py:48
  227.0 10.7 %convolution_convert_fusion.2 = bf16[1024,1536]{1,0:T(8,128)(2,1)} fusion(bf16[1024,1536]{0,1:T(8,128)(2,1)} %all-gather.6.cloned.1.call-done, bf16[1536,1536]{1,0:T(8,128)(2,1)} %param.9, bf16[1536,1536]{1,0:T(8,128)(2,1)} %mul.108), kind=kOutput, calls=%fused_computation.8 | convolution fusion | flops 4835770368 | bytes 15728640 | tf_op jit(solution)/shard_map/dot_general | solution.py:51
  237.6 0.0 reduce-scatter.9.cloned.1.call-update
  237.7 0.0 copy-start
  237.7 0.3 reduce-scatter.11.cloned.1.call-start
  238.0 50.7 %all-gather.8.cloned.1.call-done = bf16[1024,1536]{0,1:T(8,128)(2,1)} async-done(((bf16[128,1536]{0,1:T(8,128)(2,1)}), bf16[1024,1536]{0,1:T(8,128)(2,1)}) %all-gather.8.cloned.1.call-update) | async-done | bytes 3145744 | tf_op jit(solution)/shard_map/all_gather | solution.py:68
  288.7 9.4 %convolution_convert_fusion = bf16[1024,1536]{1,0:T(8,128)(2,1)} fusion(bf16[1024,1536]{0,1:T(8,128)(2,1)} %all-gather.8.cloned.1.call-done, bf16[1536,1536]{1,0:T(8,128)(2,1)} %mul.102), kind=kOutput, calls=%fused_computation.6 | convolution fusion | flops 4833411072 | bytes 11010048 | tf_op jit(solution)/shard_map/dot_general | solution.py:23
  298.1 0.0 reduce-scatter.11.cloned.1.call-update
  298.1 0.0 copy-done
  298.1 0.1 copy.16
  298.2 7.8 %mul.127 = f32[24,64,24,64]{3,2,1,0:T(8,128)} broadcast(f32[24,24]{1,0:T(8,128)S(1)} %get-tuple-element.18), dimensions={0,2} | broadcast | bytes 9439488 | tf_op jit(solution)/shard_map/mul | solution.py:14
  306.0 16.3 %mul.128 = f32[1536,1536]{1,0:T(8,128)} reshape(f32[24,64,24,64]{3,2,1,0:T(8,128)} %mul.127) | data formatting | bytes 18874368 | tf_op jit(solution)/shard_map/mul | solution.py:14
  322.3 7.9 %mul.123 = f32[24,64,24,64]{1,0,3,2:T(8,128)} broadcast(f32[24,24]{0,1:T(8,128)S(1)} %copy.16), dimensions={0,2} | broadcast | bytes 9439488 | tf_op jit(solution)/shard_map/mul | solution.py:14
  330.2 16.6 %mul.124 = f32[1536,1536]{0,1:T(8,128)} reshape(f32[24,64,24,64]{1,0,3,2:T(8,128)} %mul.123) | data formatting | bytes 18874368 | tf_op jit(solution)/shard_map/mul | solution.py:14
  346.9 10.4 %fusion.1 = bf16[1536,1536]{0,1:T(8,128)(2,1)} fusion(f32[1536,1536]{0,1:T(8,128)} %mul.124, bf16[1024,1536]{0,1:T(8,128)(2,1)} %all-gather.8.cloned.1.call-done, bf16[1024,1536]{1,0:T(8,128)(2,1)} %all-gather.4.cloned.1.call-done), kind=kOutput, calls=%fused_computation.4 | convolution fusion | flops 4838916096 | bytes 20447232 | tf_op jit(solution)/shard_map/dot_general | solution.py:29
  357.3 6.6 %copy.18 = bf16[1536,1536]{1,0:T(8,128)(2,1)} copy(bf16[1536,1536]{0,1:T(8,128)(2,1)} %fusion.1) | data formatting | bytes 9437184
  363.9 10.1 %fusion.2 = bf16[1536,1536]{1,0:T(8,128)(2,1)} fusion(f32[1536,1536]{1,0:T(8,128)} %mul.128, bf16[1024,1536]{0,1:T(8,128)(2,1)} %all-gather.6.cloned.1.call-done, bf16[1024,1536]{1,0:T(8,128)(2,1)S(1)} %bitcast.33), kind=kOutput, calls=%fused_computation.5 | convolution fusion | flops 4838916096 | bytes 20447232 | tf_op jit(solution)/shard_map/dot_general | solution.py:29
  374.0 0.0 reduce-scatter.9.cloned.1.call-done
  374.0 1.1 reshape.32
  375.1 0.7 copy.17
  375.8 19.2 %reduce-scatter.11.cloned.1.call-done = bf16[64,1536]{1,0:T(8,128)(2,1)} async-done(((bf16[1024,1536]{1,0:T(8,128)(2,1)}), bf16[64,1536]{1,0:T(8,128)(2,1)}) %reduce-scatter.11.cloned.1.call-update) | async-done | bytes 196624 | tf_op jit(solution)/shard_map/reduce_scatter | solution.py:75
  (1 shorter events, 0.0 us)
Async XLA Ops:
  8.0 94.9 %all-gather.4.cloned.1.call-start = ((), (), s32[]{:S(2)}) async-start(), calls=%async_computation.5 | async-start | bytes 3342336 | tf_op jit(solution)/shard_map/all_gather | solution.py:37
  8.7 10.1 %copy-start.1 = (s32[24,24]{1,0:T(8,128)S(1)}, s32[24,24]{1,0:T(8,128)}, u32[]{:S(2)}) copy-start(s32[24,24]{1,0:T(8,128)} %param.10) | copy-start | bytes 6916
  11.6 49.7 %all-to-all-start = ((bf16[16,64,1536]{2,1,0:T(8,128)(2,1)}), bf16[16,64,1536]{2,1,0:T(8,128)(2,1)S(1)}, u32[]{:S(2)}, u32[]{:S(2)}) async-start(bf16[16,64,1536]{2,1,0:T(8,128)(2,1)} %stack.2), calls=%async_computation.1 | async-start | bytes 6291456 | tf_op jit(solution)/shard_map/all_to_all | solution.py:60
  18.8 102.9 %reduce-scatter.15.cloned.1.call-start = ((), (), s32[]{:S(2)}) async-start(), calls=%async_computation.11 | async-start | bytes 3538944
  72.0 4.9 %copy-start.2 = (s32[24,24]{1,0:T(8,128)S(1)}, s32[24,24]{1,0:T(8,128)}, u32[]{:S(2)}) copy-start(s32[24,24]{1,0:T(8,128)} %param.8) | copy-start | bytes 6916
  76.7 93.2 %reduce-scatter.13.cloned.1.call-start = ((), (), s32[]{:S(2)}) async-start(), calls=%async_computation.10 | async-start | bytes 3538944
  117.1 109.8 %all-gather.6.cloned.1.call-start = ((), (), s32[]{:S(2)}) async-start(), calls=%async_computation.6 | async-start | bytes 3538944 | tf_op jit(solution)/shard_map/all_gather | solution.py:48
  174.4 114.2 %all-gather.8.cloned.1.call-start = ((), (), s32[]{:S(2)}) async-start(), calls=%async_computation.8 | async-start | bytes 3538944 | tf_op jit(solution)/shard_map/all_gather | solution.py:68
  175.2 198.9 %reduce-scatter.9.cloned.1.call-start = ((), (), s32[]{:S(2)}) async-start(), calls=%async_computation.7 | async-start | bytes 3342336 | tf_op jit(solution)/shard_map/reduce_scatter | solution.py:50
  237.7 60.5 %copy-start = (f32[24,24]{1,0:T(8,128)S(1)}, f32[24,24]{1,0:T(8,128)}, u32[]{:S(2)}) copy-start(f32[24,24]{1,0:T(8,128)} %get-tuple-element.20) | copy-start | bytes 6916
  237.7 157.3 %reduce-scatter.11.cloned.1.call-start = ((), (), s32[]{:S(2)}) async-start(), calls=%async_computation.9 | async-start | bytes 3342336 | tf_op jit(solution)/shard_map/reduce_scatter | solution.py:75
Sparse Core Ops, SparseCore 0:
  11.3 72.6 all-gather.3
  237.8 78.2 reduce-scatter.8
  320.8 74.1 reduce-scatter.10
Sparse Core Ops, SparseCore 1:
  76.8 44.8 reduce-scatter.14
  123.9 45.9 reduce-scatter.12
  174.5 52.4 all-gather.5
  228.5 60.0 all-gather.7
